TPU v7x, 128 devices: a whole 4x4x4 slice. The times are simulated.
128 devices in a mesh: dp: 16 (over x, z), tensor: 8 (over y, core).
Axes of the slice: x: 4, y: 4, z: 4, core: 2. Of those that a mesh axis runs over, the one named last changes fastest.
Arguments:
- attn_norm_grad: bfloat16 [16, 2048], P('dp', 'tensor'), may hold values from -1.5 to 1.5
- query_grad: bfloat16 [16, 2048, 2048], P('dp', None, 'tensor'), may hold values from -1.5 to 1.5
- forget_grad: bfloat16 [16, 2048, 2048], P('dp', None, 'tensor'), may hold values from -1.5 to 1.5
- input_grad: bfloat16 [16, 2048, 2048], P('dp', None, 'tensor'), may hold values from -1.5 to 1.5
- group_norm_grad: bfloat16 [16, 2048], P('dp', 'tensor'), may hold values from -1.5 to 1.5
- output_gate_grad: bfloat16 [16, 2048, 2048], P('dp', None, 'tensor'), may hold values from -1.5 to 1.5
- out_proj_grad: bfloat16 [16, 2048, 2048], P('dp', 'tensor'), may hold values from -1.5 to 1.5
- mlp_norm_grad: bfloat16 [16, 2048], P('dp', 'tensor'), may hold values from -1.5 to 1.5
- gate_proj_grad: bfloat16 [16, 2048, 2816], P('dp', None, 'tensor'), may hold values from -1.5 to 1.5
- up_proj_grad: bfloat16 [16, 2048, 2816], P('dp', None, 'tensor'), may hold values from -1.5 to 1.5
- down_proj_grad: bfloat16 [16, 2816, 2048], P('dp', 'tensor'), may hold values from -1.5 to 1.5
- weights: float32 [8, 4784896], P('tensor', 'dp'), as said below
- first_moment: float32 [8, 4784896], P('tensor', 'dp'), may hold values from -0.6 to 0.6
- second_moment: float32 [8, 4784896], P('tensor', 'dp'), may hold values from 0.001 to 1
Outputs:
- new_weights: float32 [8, 4784896], P('tensor', 'dp')
- new_first: float32 [8, 4784896], P('tensor', 'dp')
- new_second: float32 [8, 4784896], P('tensor', 'dp')
- attn_norm_copy: bfloat16 [2048], P('tensor')
- query_copy: bfloat16 [2048, 2048], P(None, 'tensor')
- forget_copy: bfloat16 [2048, 2048], P(None, 'tensor')
- input_copy: bfloat16 [2048, 2048], P(None, 'tensor')
- group_norm_copy: bfloat16 [2048], P('tensor')
- output_gate_copy: bfloat16 [2048, 2048], P(None, 'tensor')
- out_proj_copy: bfloat16 [2048, 2048], P('tensor')
- mlp_norm_copy: bfloat16 [2048], P('tensor')
- gate_proj_copy: bfloat16 [2048, 2816], P(None, 'tensor')
- up_proj_copy: bfloat16 [2048, 2816], P(None, 'tensor')
- down_proj_copy: bfloat16 [2816, 2048], P('tensor')
Inputs may be any that keep to these rules, and one draw needn't show every extreme that they name: float32 master weights of order one.
All inputs are finite; a program needn't handle non-finite values.
Results may differ from a plain program's by a relative error of at most 0.0085.
Values may be sent and summed in bfloat16 or wider, within the bound.
A program may use at most 192 MiB of HBM per device.

v0:
```python
import functools

import jax
import jax.numpy as jnp
from jax import lax
from jax.experimental import pallas as pl
from jax.experimental.pallas import tpu as pltpu
from jax.sharding import PartitionSpec as P

MESH = pl.DeviceIdType.MESH

GAIN_SEGMENTS = (0, 4, 7)


def apply_kernel(nd, nt, segments, weight_ref, update_ref, new_ref, low_ref, *scratch):
    recv_a, recv_b, send_a, got_a, send_b, got_b = scratch
    d = lax.axis_index("dp")
    t = lax.axis_index("tensor")
    barrier = pltpu.get_barrier_semaphore()
    for step in range(1, nt):
        pl.semaphore_signal(
            barrier, inc=1, device_id=(d, lax.rem(t + step, nt)), device_id_type=MESH
        )
    for step in range(1, nd):
        pl.semaphore_signal(
            barrier, inc=1, device_id=(lax.rem(d + step, nd), t), device_id_type=MESH
        )
    row = lax.broadcasted_iota(jnp.int32, (8, 128), 0)
    lane = lax.broadcasted_iota(jnp.int32, (8, 128), 1)

    def total(x):
        return jnp.sum(jnp.sum(x, axis=0, keepdims=True), axis=1, keepdims=True)

    def pick(vec, k):
        return total(jnp.where((row == 0) & (lane == k), vec, 0.0))

    vec = jnp.zeros((8, 128), jnp.float32)
    for k, (r0, r1, l0, l1) in enumerate(segments):
        if l0 is None:
            acc_w = jnp.zeros((8, 128), jnp.float32)
            acc_u = jnp.zeros((8, 128), jnp.float32)
            for r in range(r0, r1, 32):
                w = weight_ref[r : r + 32, :]
                u = update_ref[r : r + 32, :]
                acc_w = acc_w + jnp.sum((w * w).reshape(4, 8, 128), axis=0)
                acc_u = acc_u + jnp.sum((u * u).reshape(4, 8, 128), axis=0)
        else:
            keep = (row == 0) & (lane >= l0) & (lane < l1)
            w = weight_ref[r0 : r0 + 8, :]
            u = update_ref[r0 : r0 + 8, :]
            acc_w = jnp.where(keep, w * w, 0.0)
            acc_u = jnp.where(keep, u * u, 0.0)
        vec = jnp.where((row == 0) & (lane == k), total(acc_w), vec)
        vec = jnp.where((row == 1) & (lane == k), total(acc_u), vec)
    pl.semaphore_wait(barrier, nt - 1 + nd - 1)
    recv_a[t] = vec
    copies = []
    for step in range(1, nt):
        copy = pltpu.make_async_remote_copy(
            src_ref=recv_a.at[t],
            dst_ref=recv_a.at[t],
            send_sem=send_a.at[step],
            recv_sem=got_a.at[t],
            device_id=(d, lax.rem(t + step, nt)),
            device_id_type=MESH,
        )
        copy.start()
        copies.append(copy)
    for step in range(1, nt):
        source = lax.rem(t + nt - step, nt)
        pltpu.make_async_remote_copy(
            src_ref=recv_a.at[source],
            dst_ref=recv_a.at[source],
            send_sem=send_a.at[step],
            recv_sem=got_a.at[source],
            device_id=(d, source),
            device_id_type=MESH,
        ).wait_recv()
    for copy in copies:
        copy.wait_send()
    acc = recv_a[0]
    for slot in range(1, nt):
        acc = acc + recv_a[slot]
    recv_b[d] = acc
    copies = []
    for step in range(1, nd):
        copy = pltpu.make_async_remote_copy(
            src_ref=recv_b.at[d],
            dst_ref=recv_b.at[d],
            send_sem=send_b.at[step],
            recv_sem=got_b.at[d],
            device_id=(lax.rem(d + step, nd), t),
            device_id_type=MESH,
        )
        copy.start()
        copies.append(copy)
    for step in range(1, nd):
        source = lax.rem(d + nd - step, nd)
        pltpu.make_async_remote_copy(
            src_ref=recv_b.at[source],
            dst_ref=recv_b.at[source],
            send_sem=send_b.at[step],
            recv_sem=got_b.at[source],
            device_id=(source, t),
            device_id_type=MESH,
        ).wait_recv()
    for copy in copies:
        copy.wait_send()
    acc = recv_b[0]
    for slot in range(1, nd):
        acc = acc + recv_b[slot]
    trust = jnp.sqrt(acc[0:1, :]) / jnp.sqrt(acc[1:2, :])
    trust = jnp.broadcast_to(trust, (8, 128))
    gain_scale = jnp.zeros((8, 128), jnp.float32)
    for k, (r0, r1, l0, l1) in enumerate(segments):
        factor = 0.1 * pick(trust, k)
        if l0 is None:
            for r in range(r0, r1, 32):
                w = weight_ref[r : r + 32, :]
                u = update_ref[r : r + 32, :]
                new = w - factor * u
                new_ref[r : r + 32, :] = new
                low_ref[r : r + 32, :] = new.astype(low_ref.dtype)
        else:
            gain_scale = jnp.where((lane >= l0) & (lane < l1), factor, gain_scale)
            tail = r0
    for r in range(tail, weight_ref.shape[0], 8):
        w = weight_ref[r : r + 8, :]
        u = update_ref[r : r + 8, :]
        scale = gain_scale if r == tail else jnp.zeros((8, 128), jnp.float32)
        new = w - scale * u
        new_ref[r : r + 8, :] = new
        low_ref[r : r + 8, :] = new.astype(low_ref.dtype)


def pack_kernel(plan, *refs):
    out_ref = refs[-1]
    owners = out_ref.shape[0]

    def body(j, carry):
        for index, (r0, a, b, raw) in enumerate(plan):
            src = refs[index]
            if raw:
                start = pl.multiple_of(j * a, a)
                for rt in range(a // 8):
                    for ct in range(b // 128):
                        at = r0 + (rt * (b // 128) + ct) * 8
                        out_ref[j, at : at + 8, :] = src[
                            0, pl.ds(start + rt * 8, 8), ct * 128 : (ct + 1) * 128
                        ]
            else:
                out_ref[j, r0 : r0 + a, :] = src[j]
        return carry

    lax.fori_loop(0, owners, body, 0)


def pack_rows(inputs, plan, owners, rows):
    return pl.pallas_call(
        functools.partial(pack_kernel, plan),
        out_shape=jax.ShapeDtypeStruct((owners, rows, 128), jnp.bfloat16),
        in_specs=[pl.BlockSpec(memory_space=pltpu.VMEM)] * len(inputs),
        out_specs=pl.BlockSpec(memory_space=pltpu.VMEM),
    )(*inputs)


def apply_step(weight_p, update, segments):
    nd = lax.axis_size("dp")
    nt = lax.axis_size("tensor")
    return pl.pallas_call(
        functools.partial(apply_kernel, nd, nt, segments),
        out_shape=(
            jax.ShapeDtypeStruct(weight_p.shape, jnp.float32),
            jax.ShapeDtypeStruct(weight_p.shape, jnp.bfloat16),
        ),
        in_specs=[pl.BlockSpec(memory_space=pltpu.VMEM)] * 2,
        out_specs=(
            pl.BlockSpec(memory_space=pltpu.VMEM),
            pl.BlockSpec(memory_space=pltpu.VMEM),
        ),
        scratch_shapes=[
            pltpu.VMEM((nt, 8, 128), jnp.float32),
            pltpu.VMEM((nd, 8, 128), jnp.float32),
            pltpu.SemaphoreType.DMA((nt,)),
            pltpu.SemaphoreType.DMA((nt,)),
            pltpu.SemaphoreType.DMA((nd,)),
            pltpu.SemaphoreType.DMA((nd,)),
        ],
        compiler_params=pltpu.CompilerParams(collective_id=0, has_side_effects=True),
    )(weight_p, update)


def on_device(*args):
    grads = args[:11]
    weights, first_moment, second_moment = args[11:]
    owners = lax.axis_size("dp")
    shapes = [g.shape[1:] for g in grads]
    pieces = [g.reshape(owners, -1) for g in grads]
    piece_len = [p.shape[1] for p in pieces]
    starts = [sum(piece_len[:k]) for k in range(11)]
    order = [k for k in range(11) if k not in GAIN_SEGMENTS] + list(GAIN_SEGMENTS)
    packed_len = sum(piece_len)
    padded = -(-packed_len // 1024) * 1024
    rows = padded // 128
    blocks = [(g.shape[1] // owners, g.shape[2]) if g.ndim == 3 else None for g in grads]

    def to_rows(x, a, b):
        lead = x.shape[0]
        if a % 8 == 0 and b % 128 == 0:
            x = x.reshape(lead, a // 8, 8, b // 128, 128).transpose(0, 1, 3, 2, 4)
            return x.reshape(lead, a * b // 128, 128)
        if b % 128 != 0 and a == 128:
            return x.transpose(0, 2, 1)
        return x.reshape(lead, a * b // 128, 128)

    def from_rows(y, a, b):
        lead = y.shape[0]
        if a % 8 == 0 and b % 128 == 0:
            y = y.reshape(lead, a // 8, b // 128, 8, 128).transpose(0, 1, 3, 2, 4)
            return y.reshape(lead, a, b)
        if b % 128 != 0 and a == 128:
            return y.transpose(0, 2, 1)
        return y.reshape(lead, a, b)

    big = [k for k in order if k not in GAIN_SEGMENTS]
    inputs = []
    plan = []
    row = 0
    for k in big:
        a, b = blocks[k]
        if a % 16 == 0 and b % 128 == 0:
            inputs.append(grads[k])
            plan.append((row, a, b, True))
        else:
            inputs.append(to_rows(grads[k][0].reshape((owners,) + blocks[k]), a, b))
            plan.append((row, a * b // 128, 128, False))
        row += a * b // 128
    gains = jnp.concatenate([pieces[k] for k in GAIN_SEGMENTS], axis=1)
    gain_width = gains.shape[1]
    used_rows = row + 1
    tail = jnp.pad(gains, ((0, 0), (0, 128 - gain_width))).reshape(owners, 1, 128)
    tail = jnp.pad(tail, ((0, 0), (0, rows - used_rows), (0, 0)))
    inputs.append(tail)
    plan.append((row, rows - row, 128, False))
    flat = pack_rows(inputs, tuple(plan), owners, rows)
    summed = lax.psum_scatter(flat, "dp", scatter_dimension=0, tiled=True)
    summed = lax.optimization_barrier(summed).reshape(-1)
    packed_start = {}
    offset = 0
    for k in order:
        packed_start[k] = offset
        offset += piece_len[k]
    segments = []
    for k in range(11):
        a, b = packed_start[k], packed_start[k] + piece_len[k]
        if a % 128 == 0 and b % 128 == 0:
            segments.append((a // 128, b // 128, None, None))
        else:
            segments.append((a // 128, a // 128 + 1, a % 128, (b - 1) % 128 + 1))

    def to_packed(row):
        out = []
        for k in big:
            seg = row[starts[k] : starts[k] + piece_len[k]].reshape((1,) + blocks[k])
            out.append(to_rows(seg, *blocks[k])[0])
        tail = [row[starts[k] : starts[k] + piece_len[k]] for k in GAIN_SEGMENTS]
        tail.append(jnp.zeros((128 - gain_width,), row.dtype))
        out.append(jnp.concatenate(tail).reshape(1, 128))
        out.append(jnp.zeros((rows - used_rows, 128), row.dtype))
        return jnp.concatenate(out, axis=0)

    def to_flat(block):
        out = []
        for k in range(11):
            r0, r1, l0, l1 = segments[k]
            if l0 is None:
                seg = from_rows(block[r0:r1].reshape(1, r1 - r0, 128), *blocks[k])
                out.append(seg.reshape(-1))
            else:
                out.append(block[r0, l0:l1])
        return jnp.concatenate(out).reshape(1, -1)

    grad = summed.reshape(rows, 128).astype(jnp.float32)
    weight_p = to_packed(weights.reshape(-1))
    first_p = to_packed(first_moment.reshape(-1))
    second_p = to_packed(second_moment.reshape(-1))
    new_first = 0.9 * first_p + 0.1 * grad
    new_second = 0.999 * second_p + 0.001 * grad * grad
    position = (
        lax.broadcasted_iota(jnp.int32, (rows, 128), 0) * 128
        + lax.broadcasted_iota(jnp.int32, (rows, 128), 1)
    )
    big_end = min(packed_start[k] for k in GAIN_SEGMENTS)
    update = new_first / (jnp.sqrt(new_second) + 1e-06)
    update = jnp.where(position < big_end, update + 0.01 * weight_p, update)
    new_weights, rounded = apply_step(weight_p, update, tuple(segments))
    gathered = lax.all_gather(rounded, "dp", axis=0, tiled=False)
    copies = [None] * 11
    for k in range(11):
        r0, r1, l0, l1 = segments[k]
        if l0 is None:
            part = from_rows(gathered[:, r0:r1, :], *blocks[k])
        else:
            part = gathered[:, r0, l0:l1]
        copies[k] = part.reshape(shapes[k])
    return (
        to_flat(new_weights),
        to_flat(new_first),
        to_flat(new_second),
        *copies,
    )


def solution(mesh):
    return jax.shard_map(
        on_device,
        mesh=mesh,
        in_specs=(
            P("dp", "tensor"),
            P("dp", None, "tensor"),
            P("dp", None, "tensor"),
            P("dp", None, "tensor"),
            P("dp", "tensor"),
            P("dp", None, "tensor"),
            P("dp", "tensor", None),
            P("dp", "tensor"),
            P("dp", None, "tensor"),
            P("dp", None, "tensor"),
            P("dp", "tensor", None),
            P("tensor", "dp"),
            P("tensor", "dp"),
            P("tensor", "dp"),
        ),
        out_specs=(
            P("tensor", "dp"),
            P("tensor", "dp"),
            P("tensor", "dp"),
            P("tensor"),
            P(None, "tensor"),
            P(None, "tensor"),
            P(None, "tensor"),
            P("tensor"),
            P(None, "tensor"),
            P("tensor", None),
            P("tensor"),
            P(None, "tensor"),
            P(None, "tensor"),
            P("tensor", None),
        ),
        check_vma=False,
    )
```

profile of v0, /device:TPU:1, one launch (start us, length us, event | category | flops | bytes accessed | tf_op | source)
XLA Modules:
  0.0 262.3 jit_solution(15883913036351235822)
XLA Ops:
  7.2 1.8 copy.151
  9.1 0.3 copy.150
  9.5 3.5 %reshape_reshape_squeeze.3.refs_7_ = bf16[16,352,128]{2,1,0:T(8,128)(2,1)} reshape(bf16[1,352,2048]{2,1,0:T(8,128)(2,1)} %param.24) | data formatting | bytes 2883584 | tf_op jit(solution)/shard_map/reshape;reshape;squeeze | solution.py:214
  13.4 2.3 copy_bitcast_fusion.2
  15.7 0.6 pad.9.refs_8_
  16.4 8.4 %shard_map.245 = bf16[16,2344,128]{2,1,0:T(8,128)(2,1)} custom-call(bf16[1,2048,256]{2,1,0:T(8,128)(2,1)} %refs_0_.1, bf16[1,2048,256]{2,1,0:T(8,128)(2,1)} %refs_1_.1, bf16[1,2048,256]{2,1,0:T(8,128)(2,1)} %refs_2_.1, bf16[1,2048,256]{2,1,0:T(8,128)(2,1)} %refs_3_.1, bf16[1,256,2048]{2,1,0:T(8,128)(2,1)} %refs_4_.1, ...), custom_call_target="tpu_custom_call" | custom-call | tf_op jit(solution)/shard_map/pallas_call | solution.py:159
  24.8 1.2 copy-done.4
  26.0 1.4 fusion.20
  27.4 0.7 copy.95
  28.1 0.7 copy.96
  28.8 0.7 copy.97
  29.4 0.7 copy.98
  30.1 0.7 copy.99
  30.8 1.9 slice_reduce_fusion.4
  33.0 0.8 copy.101
  33.8 1.4 fusion.19
  35.3 0.7 copy.112
  35.9 0.7 copy.113
  36.6 0.6 copy.114
  37.2 0.7 copy.115
  37.9 0.7 copy.116
  38.6 4.2 %slice_reduce_fusion = (f32[45056]{0:T(1024)S(1)}, f32[45056]{0:T(1024)S(1)}, f32[1,45056]{1,0:T(1,128)}, f32[1,45056]{1,0:T(1,128)}, f32[45056]{0:T(1024)S(1)}, /*index=5*/f32[45056]{0:T(1024)S(1)}) fusion(f32[1,299056]{1,0:T(1,128)S(1)} %copy-done.5, f32[1,299056]{1,0:T(1,128)} %param.26), kind=kLoop, calls=%fused_computation.22 | loop fusion | bytes 2162688 | tf_op jit(solution)/shard_map/slice | solution.py:264
  43.2 0.8 copy.118
  44.0 2.6 fusion.18
  46.6 0.7 copy.102
  47.3 0.7 copy.103
  47.9 0.7 copy.104
  48.6 0.7 copy.105
  49.3 0.7 copy.106
  50.5 0.8 slice_bitcast_fusion.22
  51.4 5.6 %concatenate.31.weight_ref = f32[2344,128]{1,0:T(8,128)S(1)} concatenate(f32[256,128]{1,0:T(8,128)} %bitcast.342, f32[256,128]{1,0:T(8,128)} %bitcast.343, f32[256,128]{1,0:T(8,128)} %bitcast.344, f32[256,128]{1,0:T(8,128)} %bitcast.345, f32[256,128]{1,0:T(8,128)} %bitcast.346, f32[352,128]{1,0:T(8,128)S(1)} %bitcast.288, f32[352,128]{1,0:T(8,128)S(1)} %bitcast.289, ...), dimensions={0} | concatenate | bytes 2400256 | tf_op jit(solution)/shard_map/concatenate | solution.py:270
  57.0 6.0 %concatenate.36 = f32[2344,128]{1,0:T(8,128)S(1)} concatenate(f32[256,128]{1,0:T(8,128)} %bitcast.347, f32[256,128]{1,0:T(8,128)} %bitcast.348, f32[256,128]{1,0:T(8,128)} %bitcast.349, f32[256,128]{1,0:T(8,128)} %bitcast.350, f32[256,128]{1,0:T(8,128)} %bitcast.351, f32[352,128]{1,0:T(8,128)S(1)} %bitcast.290, f32[352,128]{1,0:T(8,128)S(1)} %bitcast.291, f32[352,128]{1,0:T(8,128)} %bitcast.296, ...), dimensions={0} | concatenate | bytes 2400256 | tf_op jit(solution)/shard_map/concatenate | solution.py:270
  63.1 9.6 %concatenate.33 = f32[2344,128]{1,0:T(8,128)} concatenate(f32[256,128]{1,0:T(8,128)S(1)} %bitcast.352, f32[256,128]{1,0:T(8,128)} %bitcast.353, f32[256,128]{1,0:T(8,128)} %bitcast.354, f32[256,128]{1,0:T(8,128)} %bitcast.355, f32[256,128]{1,0:T(8,128)} %bitcast.356, f32[352,128]{1,0:T(8,128)S(1)} %bitcast.292, f32[352,128]{1,0:T(8,128)S(1)} %bitcast.293, ...), dimensions={0} | concatenate | bytes 2400256 | tf_op jit(solution)/shard_map/concatenate | solution.py:270
  72.7 70.8 %reduce-scatter.4.cloned.1.call-done = bf16[1,2344,128]{2,1,0:T(8,128)(2,1)} async-done(((bf16[16,2344,128]{2,1,0:T(8,128)(2,1)}), bf16[1,2344,128]{2,1,0:T(8,128)(2,1)}) %reduce-scatter.4.cloned.1.call-update) | async-done | bytes 600080
  143.5 3.7 %add_select_fusion = (f32[2344,128]{1,0:T(8,128)}, f32[2344,128]{1,0:T(8,128)}, f32[2344,128]{1,0:T(8,128)}) fusion(f32[2344,128]{1,0:T(8,128)S(1)} %concatenate.31.weight_ref, s32[2344]{0:T(1024)S(1)} %iota_multiply_fusion, bf16[1,2344,128]{2,1,0:T(8,128)(2,1)} %reduce-scatter.4.cloned.1.call-done, f32[2344,128]{1,0:T(8,128)S(1)} %concatenate.36, ...), kind=kLoop, calls=%fused_computation.3 | loop fusion | flops 4500480 | bytes 7810208 | tf_op jit(solution)/shard_map/jit(_where)/select_n | solution.py:295
  147.2 16.6 %shard_map.246 = (f32[2344,128]{1,0:T(8,128)}, bf16[2344,128]{1,0:T(8,128)(2,1)}) custom-call(f32[2344,128]{1,0:T(8,128)} %copy-done, f32[2344,128]{1,0:T(8,128)} %get-tuple-element.27.update_ref), custom_call_target="tpu_custom_call" | custom-call | tf_op jit(solution)/shard_map/pallas_call | solution.py:170
  163.8 1.2 fusion.17
  165.4 1.1 slice_bitcast_fusion.8
  166.5 0.1 copy.124
  166.7 0.2 reshape.209
  166.8 0.1 copy.125
  167.0 0.2 reshape.211
  167.1 0.9 slice_bitcast_fusion.17
  168.0 7.0 %concatenate.37 = f32[299056]{0:T(1024)S(1)} concatenate(f32[16]{0:T(128)S(1)} %get-tuple-element.65, f32[32768]{0:T(1024)S(1)} %bitcast.297, f32[32768]{0:T(1024)S(1)} %bitcast.300, f32[32768]{0:T(1024)S(1)} %bitcast.303, f32[16]{0:T(128)S(1)} %get-tuple-element.64, f32[32768]{0:T(1024)S(1)} %bitcast.306, f32[32768]{0:T(1024)S(1)} %bitcast.309, f32[16]{0:T(128)S(1)} %get-tuple-element.63, ...), dimensions={0} | concatenate | bytes 2392448 | tf_op jit(solution)/shard_map/concatenate | solution.py:281
  175.0 6.3 %reshape.212 = f32[1,299056]{1,0:T(1,128)} reshape(f32[299056]{0:T(1024)S(1)} %concatenate.37) | data formatting | bytes 2392448 | tf_op jit(solution)/shard_map/reshape | solution.py:281
  181.7 0.7 copy.130
  182.6 0.2 reshape.214
  182.9 0.2 reshape.216
  183.1 8.1 %concatenate.38 = f32[299056]{0:T(1024)S(1)} concatenate(f32[16]{0:T(128)S(1)} %get-tuple-element.54, f32[32768]{0:T(1024)S(1)} %bitcast.298, f32[32768]{0:T(1024)S(1)} %bitcast.301, f32[32768]{0:T(1024)S(1)} %bitcast.304, f32[16]{0:T(128)S(1)} %get-tuple-element.53, f32[32768]{0:T(1024)S(1)} %bitcast.307, f32[32768]{0:T(1024)} %bitcast.310, f32[16]{0:T(128)S(1)} %get-tuple-element.52, ...), dimensions={0} | concatenate | bytes 2392448 | tf_op jit(solution)/shard_map/concatenate | solution.py:281
  191.2 6.3 %reshape.217 = f32[1,299056]{1,0:T(1,128)} reshape(f32[299056]{0:T(1024)S(1)} %concatenate.38) | data formatting | bytes 2392448 | tf_op jit(solution)/shard_map/reshape | solution.py:281
  198.1 0.2 reshape.219
  198.4 0.2 reshape.221
  198.7 7.0 %concatenate.39 = f32[299056]{0:T(1024)S(1)} concatenate(f32[16]{0:T(128)S(1)} %get-tuple-element.43, f32[32768]{0:T(1024)S(1)} %bitcast.299, f32[32768]{0:T(1024)S(1)} %bitcast.302, f32[32768]{0:T(1024)S(1)} %bitcast.305, f32[16]{0:T(128)S(1)} %get-tuple-element.42, f32[32768]{0:T(1024)S(1)} %bitcast.308, f32[32768]{0:T(1024)S(1)} %bitcast.311, f32[16]{0:T(128)S(1)} %get-tuple-element.41, ...), dimensions={0} | concatenate | bytes 2392448 | tf_op jit(solution)/shard_map/concatenate | solution.py:281
  205.7 6.3 %reshape.222 = f32[1,299056]{1,0:T(1,128)} reshape(f32[299056]{0:T(1024)S(1)} %concatenate.39) | data formatting | bytes 2392448 | tf_op jit(solution)/shard_map/reshape | solution.py:281
  212.0 26.2 %all-gather.3.cloned.1.call-done = bf16[37504,128]{1,0:T(8,128)(2,1)} async-done(((bf16[2344,128]{1,0:T(8,128)(2,1)}), bf16[37504,128]{1,0:T(8,128)(2,1)}) %all-gather.3.cloned.1.call-update) | async-done | bytes 9601040 | tf_op jit(solution)/shard_map/all_gather | solution.py:297
  238.2 1.0 slice_reduce_fusion.6
  239.2 5.0 %fusion.14 = (bf16[16,256,128]{2,1,0:T(8,128)(2,1)}, bf16[16,256,128]{2,1,0:T(8,128)(2,1)}, bf16[16,256,128]{2,1,0:T(8,128)(2,1)}, bf16[16,256,128]{2,1,0:T(8,128)(2,1)}, bf16[16,256,128]{2,1,0:T(8,128)(2,1)}) fusion(bf16[16,2344,128]{2,1,0:T(8,128)(2,1)} %bitcast.275), kind=kLoop, calls=%fused_computation.64 | loop fusion | bytes 10485760 | tf_op jit(solution)/shard_map/slice | solution.py:302
  244.2 3.7 %fusion.13 = (bf16[16,352,128]{2,1,0:T(8,128)(2,1)S(1)}, bf16[16,44,8,128]{3,2,1,0:T(8,128)(2,1)}, bf16[16,44,8,128]{3,2,1,0:T(8,128)(2,1)S(1)}) fusion(bf16[16,2344,128]{2,1,0:T(8,128)(2,1)} %bitcast.276), kind=kLoop, calls=%fused_computation.63 | loop fusion | bytes 8650752 | tf_op jit(solution)/shard_map/slice | solution.py:302
  247.8 0.6 reshape_squeeze.17
  248.4 0.6 reshape_squeeze.18
  249.0 0.6 reshape_squeeze.19
  249.6 2.9 %copy.157 = bf16[16,44,8,128]{3,2,0,1:T(8,128)(2,1)} copy(bf16[16,44,8,128]{3,2,1,0:T(8,128)(2,1)} %get-tuple-element.31) | data formatting | bytes 2883584 | tf_op jit(solution)/shard_map/reshape | solution.py:305
  252.5 1.5 copy.156
  254.0 1.5 reshape_reshape.204
  (76 shorter events, 3.6 us)
Async XLA Ops:
  7.2 136.3 %reduce-scatter.4.cloned.1.call-start = ((), (), s32[]{:S(2)}) async-start(), calls=%async_computation.2 | async-start | bytes 10201088
  7.2 1.8 copy-start.3
  9.4 3.6 %copy-start.10 = (bf16[1,256]{1,0:T(2,128)(2,1)S(1)}, bf16[1,256]{1,0:T(2,128)(2,1)}, u32[]{:S(2)}) copy-start(bf16[1,256]{1,0:T(2,128)(2,1)} %param.21) | copy-start | bytes 1540
  9.4 3.7 %copy-start.11 = (bf16[1,256]{1,0:T(2,128)(2,1)S(1)}, bf16[1,256]{1,0:T(2,128)(2,1)}, u32[]{:S(2)}) copy-start(bf16[1,256]{1,0:T(2,128)(2,1)} %param.18) | copy-start | bytes 1540
  9.4 3.8 %copy-start.12 = (bf16[1,256]{1,0:T(2,128)(2,1)S(1)}, bf16[1,256]{1,0:T(2,128)(2,1)}, u32[]{:S(2)}) copy-start(bf16[1,256]{1,0:T(2,128)(2,1)} %param.14) | copy-start | bytes 1540
  24.7 1.3 copy-start.4
  24.8 213.5 %all-gather.3.cloned.1.call-start = ((), (), s32[]{:S(2)}) async-start(), calls=%async_computation.1 | async-start | bytes 10201088 | tf_op jit(solution)/shard_map/all_gather | solution.py:297
  30.8 3.1 %copy-start.5 = (f32[1,299056]{1,0:T(1,128)S(1)}, f32[1,299056]{1,0:T(1,128)}, u32[]{:S(2)}) copy-start(f32[1,299056]{1,0:T(1,128)} %param.27) | copy-start | bytes 3588676
  47.9 3.5 %copy-start.6 = (f32[1,128,352]{1,2,0:T(8,128)S(1)}, f32[1,128,352]{1,2,0:T(8,128)}, u32[]{:S(2)}) copy-start(f32[1,128,352]{1,2,0:T(8,128)} %copy.101) | copy-start | bytes 540676
  51.4 5.6 %copy-start.7 = (f32[1,128,352]{1,2,0:T(8,128)S(1)}, f32[1,128,352]{1,2,0:T(8,128)}, u32[]{:S(2)}) copy-start(f32[1,128,352]{1,2,0:T(8,128)} %copy.118) | copy-start | bytes 540676
  57.0 86.5 %copy-start = (f32[2344,128]{1,0:T(8,128)}, f32[2344,128]{1,0:T(8,128)S(1)}, u32[]{:S(2)}) copy-start(f32[2344,128]{1,0:T(8,128)S(1)} %concatenate.31.weight_ref) | copy-start | bytes 3600388
  57.0 6.0 %copy-start.8 = (f32[1,45056]{1,0:T(1,128)S(1)}, f32[1,45056]{1,0:T(1,128)}, u32[]{:S(2)}) copy-start(f32[1,45056]{1,0:T(1,128)} %get-tuple-element.101) | copy-start | bytes 540676
  57.0 6.0 %copy-start.9 = (f32[1,16,8,2,128]{4,2,3,1,0:T(8,128)S(1)}, f32[1,16,8,2,128]{4,2,3,1,0:T(8,128)}, u32[]{:S(2)}) copy-start(f32[1,16,8,2,128]{4,2,3,1,0:T(8,128)} %copy.102) | copy-start | bytes 393220
  175.0 6.3 %copy-start.2 = (f32[2344,128]{1,0:T(8,128)S(1)}, f32[2344,128]{1,0:T(8,128)}, u32[]{:S(2)}) copy-start(f32[2344,128]{1,0:T(8,128)} %get-tuple-element.29) | copy-start | bytes 3600388
  191.2 6.3 %copy-start.1 = (f32[2344,128]{1,0:T(8,128)S(1)}, f32[2344,128]{1,0:T(8,128)}, u32[]{:S(2)}) copy-start(f32[2344,128]{1,0:T(8,128)} %get-tuple-element.28) | copy-start | bytes 3600388
Sparse Core Ops, SparseCore 0:
  24.9 118.5 reduce-scatter.3
  164.0 74.2 all-gather.2
where the time goes:
time: 263 us; the launch traced here: 262 us
  local copies, waits for them, and re-layouts  122 us (46%)
  waiting for transfers between devices  97 us (37%)
  Pallas kernels  25 us (10%)
  between operations  14.5 us (6%)
  other arithmetic  3.92 us (1%)
    unnamed x3, waiting for transfers between devices  70.8 us
    all_gather x1, waiting for transfers between devices, on_device(): gathered = lax.all_gather(rounded, 'dp', axis=0, tiled=False)  26.2 us
    concatenate x3, local copies, waits for them, and re-layouts, to_flat(): return jnp.concatenate(out).reshape(1, -1)  22.1 us
    concatenate x3, local copies, waits for them, and re-layouts, to_packed(): return jnp.concatenate(out, axis=0)  21.2 us
    reshape x3, local copies, waits for them, and re-layouts, to_flat(): return jnp.concatenate(out).reshape(1, -1)  19 us
    pallas_call x1, Pallas kernels, apply_step(): pl.pallas_call(functools.partial(apply_kernel, nd, nt, segments), out_sha...  16.6 us
    slice x5, local copies, waits for them, and re-layouts, to_packed(): seg = row[starts[k]:starts[k] + piece_len[k]].reshape((1,) + blocks[k])  11.5 us
    another operation x15, local copies, waits for them, and re-layouts, to_rows(): x = x.reshape(lead, a // 8, 8, b // 128, 128).transpose(0, 1, 3, 2, 4)  10.1 us
  transfers between devices with their start and end apart: 2, of which 2 were waited for; matrix products, arithmetic and copies ran while one was open for 36% of the time, Pallas kernels for 0%

commit v1 on v0

--- a/solution.py
+++ b/solution.py
@@ -294,6 +294,9 @@
     update = new_first / (jnp.sqrt(new_second) + 1e-06)
     update = jnp.where(position < big_end, update + 0.01 * weight_p, update)
     new_weights, rounded = apply_step(weight_p, update, tuple(segments))
+    _, first_p, second_p, grad = lax.optimization_barrier((rounded, first_p, second_p, grad))
+    new_first = 0.9 * first_p + 0.1 * grad
+    new_second = 0.999 * second_p + 0.001 * grad * grad
     gathered = lax.all_gather(rounded, "dp", axis=0, tiled=False)
     copies = [None] * 11
     for k in range(11):

time: 263 us -> 263 us (level)
  waiting for transfers between devices: 97 us -> 89.3 us
  local copies, waits for them, and re-layouts: 122 us -> 128 us
    all_gather x1, waiting for transfers between devices: 26.2 us -> 12.7 us  [on_device(): gathered = lax.all_gather(rounded, 'dp', axis=0, tiled=False)]
    concatenate x3, local copies, waits for them, and re-layouts: 22.1 us -> 31.6 us  [to_flat(): return jnp.concatenate(out).reshape(1, -1)]
    concatenate x3, local copies, waits for them, and re-layouts: 21.2 us -> 14.5 us  [to_packed(): return jnp.concatenate(out, axis=0)]
    unnamed x3, waiting for transfers between devices: 70.8 us -> 76.6 us
  transfers between devices with their start and end apart: 2 -> 2, of which waited for: 2 -> 2; matrix products, arithmetic and copies ran while one was open for 36% -> 38% of each run, Pallas kernels for 0% -> 0%
where the time goes in v1:
time: 263 us; the launch traced here: 262 us
  local copies, waits for them, and re-layouts  128 us (49%)
  waiting for transfers between devices  89.3 us (34%)
  Pallas kernels  25 us (10%)
  between operations  14.5 us (6%)
  other arithmetic  4.99 us (2%)
    unnamed x3, waiting for transfers between devices  76.6 us
    concatenate x3, local copies, waits for them, and re-layouts, to_flat(): return jnp.concatenate(out).reshape(1, -1)  31.6 us
    reshape x3, local copies, waits for them, and re-layouts, to_flat(): return jnp.concatenate(out).reshape(1, -1)  18.8 us
    pallas_call x1, Pallas kernels, apply_step(): pl.pallas_call(functools.partial(apply_kernel, nd, nt, segments), out_sha...  16.6 us
    concatenate x3, local copies, waits for them, and re-layouts, to_packed(): return jnp.concatenate(out, axis=0)  14.5 us
    all_gather x1, waiting for transfers between devices, on_device(): gathered = lax.all_gather(rounded, 'dp', axis=0, tiled=False)  12.7 us
    slice x5, local copies, waits for them, and re-layouts, to_packed(): seg = row[starts[k]:starts[k] + piece_len[k]].reshape((1,) + blocks[k])  11.5 us
    another operation x15, local copies, waits for them, and re-layouts, to_rows(): x = x.reshape(lead, a // 8, 8, b // 128, 128).transpose(0, 1, 3, 2, 4)  10 us
  transfers between devices with their start and end apart: 2, of which 2 were waited for; matrix products, arithmetic and copies ran while one was open for 38% of the time, Pallas kernels for 0%

profile of v1, /device:TPU:1, one launch (start us, length us, event | category | flops | bytes accessed | tf_op | source)
XLA Modules:
  0.0 261.9 jit_solution(4077980417197412730)
XLA Ops:
  7.2 1.8 copy.151
  9.1 0.3 copy.150
  9.5 3.5 %reshape_reshape_squeeze.3.refs_7_ = bf16[16,352,128]{2,1,0:T(8,128)(2,1)} reshape(bf16[1,352,2048]{2,1,0:T(8,128)(2,1)} %param.24) | data formatting | bytes 2883584 | tf_op jit(solution)/shard_map/reshape;reshape;squeeze | solution.py:214
  13.4 2.3 copy_bitcast_fusion.2
  15.7 0.6 pad.9.refs_8_
  16.4 8.3 %shard_map.245 = bf16[16,2344,128]{2,1,0:T(8,128)(2,1)} custom-call(bf16[1,2048,256]{2,1,0:T(8,128)(2,1)} %refs_0_.1, bf16[1,2048,256]{2,1,0:T(8,128)(2,1)} %refs_1_.1, bf16[1,2048,256]{2,1,0:T(8,128)(2,1)} %refs_2_.1, bf16[1,2048,256]{2,1,0:T(8,128)(2,1)} %refs_3_.1, bf16[1,256,2048]{2,1,0:T(8,128)(2,1)} %refs_4_.1, ...), custom_call_target="tpu_custom_call" | custom-call | tf_op jit(solution)/shard_map/pallas_call | solution.py:159
  24.8 1.2 copy-done.4
  26.0 1.4 fusion.21
  27.4 0.7 copy.95
  28.1 0.7 copy.96
  28.7 0.7 copy.97
  29.4 0.7 copy.98
  30.1 0.7 copy.99
  30.8 1.9 slice_reduce_fusion.4
  33.0 0.8 copy.101
  33.8 1.4 fusion.20
  35.2 0.7 copy.112
  35.9 0.7 copy.113
  36.5 0.7 copy.114
  37.2 0.7 copy.115
  37.9 0.7 copy.116
  38.6 4.2 %slice_reduce_fusion = (f32[45056]{0:T(1024)S(1)}, f32[45056]{0:T(1024)S(1)}, f32[1,45056]{1,0:T(1,128)}, f32[1,45056]{1,0:T(1,128)}, f32[45056]{0:T(1024)S(1)}, /*index=5*/f32[45056]{0:T(1024)S(1)}) fusion(f32[1,299056]{1,0:T(1,128)S(1)} %copy-done.5, f32[1,299056]{1,0:T(1,128)} %param.26), kind=kLoop, calls=%fused_computation.26 | loop fusion | bytes 2162688 | tf_op jit(solution)/shard_map/slice | solution.py:264
  43.2 0.8 copy.118
  44.0 2.6 fusion.19
  46.5 0.7 copy.102
  47.2 0.7 copy.103
  47.9 0.7 copy.104
  48.6 0.6 copy.105
  49.2 0.7 copy.106
  50.5 0.8 slice_bitcast_fusion.22
  51.4 11.5 %concatenate.31.weight_ref = f32[2344,128]{1,0:T(8,128)} concatenate(f32[256,128]{1,0:T(8,128)} %bitcast.341, f32[256,128]{1,0:T(8,128)} %bitcast.342, f32[256,128]{1,0:T(8,128)} %bitcast.343, f32[256,128]{1,0:T(8,128)} %bitcast.344, f32[256,128]{1,0:T(8,128)} %bitcast.345, f32[352,128]{1,0:T(8,128)S(1)} %bitcast.287, f32[352,128]{1,0:T(8,128)S(1)} %bitcast.288, ...), dimensions={0} | concatenate | bytes 2400256 | tf_op jit(solution)/shard_map/concatenate | solution.py:270
  63.1 0.8 copy-done.8
  64.0 2.8 %concatenate.33 = f32[2344,128]{1,0:T(8,128)S(1)} concatenate(f32[256,128]{1,0:T(8,128)S(1)} %bitcast.351, f32[256,128]{1,0:T(8,128)S(1)} %bitcast.352, f32[256,128]{1,0:T(8,128)} %bitcast.353, f32[256,128]{1,0:T(8,128)} %bitcast.354, f32[256,128]{1,0:T(8,128)} %bitcast.355, f32[352,128]{1,0:T(8,128)S(1)} %bitcast.291, f32[352,128]{1,0:T(8,128)S(1)} %bitcast.292, ...), dimensions={0} | concatenate | bytes 2400256 | tf_op jit(solution)/shard_map/concatenate | solution.py:270
  66.9 76.6 %reduce-scatter.4.cloned.1.call-done = bf16[1,2344,128]{2,1,0:T(8,128)(2,1)} async-done(((bf16[16,2344,128]{2,1,0:T(8,128)(2,1)}), bf16[1,2344,128]{2,1,0:T(8,128)(2,1)}) %reduce-scatter.4.cloned.1.call-update) | async-done | bytes 600080
  143.4 3.3 %add_select_fusion.update_ref = f32[2344,128]{1,0:T(8,128)} fusion(f32[2344,128]{1,0:T(8,128)} %concatenate.31.weight_ref, f32[2344,128]{1,0:T(8,128)S(1)} %concatenate.36, f32[2344,128]{1,0:T(8,128)S(1)} %concatenate.33, s32[2344]{0:T(1024)S(1)} %iota_multiply_fusion, bf16[1,2344,128]{2,1,0:T(8,128)(2,1)} %reduce-scatter.4.cloned.1.call-done), kind=kLoop, calls=%fused_computation.1 | loop fusion | flops 4500480 | bytes 5409952 | tf_op jit(solution)/shard_map/jit(_where)/select_n | solution.py:295
  146.7 16.6 %shard_map.246 = (f32[2344,128]{1,0:T(8,128)}, bf16[2344,128]{1,0:T(8,128)(2,1)}) custom-call(f32[2344,128]{1,0:T(8,128)} %concatenate.31.weight_ref, f32[2344,128]{1,0:T(8,128)} %add_select_fusion.update_ref), custom_call_target="tpu_custom_call" | custom-call | tf_op jit(solution)/shard_map/pallas_call | solution.py:170
  163.4 1.2 fusion.18
  164.8 0.7 copy.122
  165.6 0.7 copy.123
  166.2 1.1 slice_bitcast_fusion.8
  167.5 0.2 reshape.209
  167.8 0.2 reshape.211
  168.0 0.9 slice_bitcast_fusion.17
  168.8 16.3 %concatenate.37 = f32[299056]{0:T(1024)} concatenate(f32[16]{0:T(128)S(1)} %get-tuple-element.70, f32[32768]{0:T(1024)S(1)} %bitcast.296, f32[32768]{0:T(1024)S(1)} %bitcast.299, f32[32768]{0:T(1024)S(1)} %bitcast.302, f32[16]{0:T(128)S(1)} %get-tuple-element.69, f32[32768]{0:T(1024)} %bitcast.305, f32[32768]{0:T(1024)} %bitcast.308, f32[16]{0:T(128)S(1)} %get-tuple-element.68, ...), dimensions={0} | concatenate | bytes 2392448 | tf_op jit(solution)/shard_map/concatenate | solution.py:281
  185.1 6.2 %reshape.212 = f32[1,299056]{1,0:T(1,128)} reshape(f32[299056]{0:T(1024)} %concatenate.37) | data formatting | bytes 2392448 | tf_op jit(solution)/shard_map/reshape | solution.py:281
  191.4 1.4 fusion.4
  193.2 0.6 copy-done.1
  194.3 0.2 reshape.216
  194.5 0.9 slice_bitcast_fusion.14
  195.3 7.0 %concatenate.38 = f32[299056]{0:T(1024)S(1)} concatenate(f32[16]{0:T(128)S(1)} %get-tuple-element.59, f32[32768]{0:T(1024)S(1)} %bitcast.297, f32[32768]{0:T(1024)S(1)} %bitcast.300, f32[32768]{0:T(1024)S(1)} %bitcast.303, f32[16]{0:T(128)S(1)} %get-tuple-element.58, f32[32768]{0:T(1024)S(1)} %bitcast.306, f32[32768]{0:T(1024)S(1)} %bitcast.309, f32[16]{0:T(128)S(1)} %get-tuple-element.57, ...), dimensions={0} | concatenate | bytes 2392448 | tf_op jit(solution)/shard_map/concatenate | solution.py:281
  202.4 6.3 %reshape.217 = f32[1,299056]{1,0:T(1,128)} reshape(f32[299056]{0:T(1024)S(1)} %concatenate.38) | data formatting | bytes 2392448 | tf_op jit(solution)/shard_map/reshape | solution.py:281
  209.1 0.7 copy.137
  210.5 8.3 %concatenate.39 = f32[299056]{0:T(1024)S(1)} concatenate(f32[16]{0:T(128)S(1)} %get-tuple-element.46, f32[32768]{0:T(1024)S(1)} %bitcast.298, f32[32768]{0:T(1024)S(1)} %bitcast.301, f32[32768]{0:T(1024)S(1)} %bitcast.304, f32[16]{0:T(128)S(1)} %get-tuple-element.45, f32[32768]{0:T(1024)S(1)} %bitcast.307, f32[32768]{0:T(1024)} %bitcast.310, f32[16]{0:T(128)S(1)} %get-tuple-element.44, ...), dimensions={0} | concatenate | bytes 2392448 | tf_op jit(solution)/shard_map/concatenate | solution.py:281
  218.8 6.3 %reshape.222 = f32[1,299056]{1,0:T(1,128)} reshape(f32[299056]{0:T(1024)S(1)} %concatenate.39) | data formatting | bytes 2392448 | tf_op jit(solution)/shard_map/reshape | solution.py:281
  225.1 12.7 %all-gather.3.cloned.1.call-done = bf16[37504,128]{1,0:T(8,128)(2,1)} async-done(((bf16[2344,128]{1,0:T(8,128)(2,1)}), bf16[37504,128]{1,0:T(8,128)(2,1)}) %all-gather.3.cloned.1.call-update) | async-done | bytes 9601040 | tf_op jit(solution)/shard_map/all_gather | solution.py:300
  237.8 1.0 slice_reduce_fusion.6
  238.8 5.0 %fusion.15 = (bf16[16,256,128]{2,1,0:T(8,128)(2,1)}, bf16[16,256,128]{2,1,0:T(8,128)(2,1)}, bf16[16,256,128]{2,1,0:T(8,128)(2,1)}, bf16[16,256,128]{2,1,0:T(8,128)(2,1)}, bf16[16,256,128]{2,1,0:T(8,128)(2,1)}) fusion(bf16[16,2344,128]{2,1,0:T(8,128)(2,1)} %bitcast.274), kind=kLoop, calls=%fused_computation.68 | loop fusion | bytes 10485760 | tf_op jit(solution)/shard_map/slice | solution.py:305
  243.7 3.7 %fusion.14 = (bf16[16,352,128]{2,1,0:T(8,128)(2,1)S(1)}, bf16[16,44,8,128]{3,2,1,0:T(8,128)(2,1)}, bf16[16,44,8,128]{3,2,1,0:T(8,128)(2,1)S(1)}) fusion(bf16[16,2344,128]{2,1,0:T(8,128)(2,1)} %bitcast.275), kind=kLoop, calls=%fused_computation.67 | loop fusion | bytes 8650752 | tf_op jit(solution)/shard_map/slice | solution.py:305
  247.4 0.6 reshape_squeeze.17
  248.0 0.6 reshape_squeeze.18
  248.6 0.6 reshape_squeeze.19
  249.2 2.9 %copy.157 = bf16[16,44,8,128]{3,2,0,1:T(8,128)(2,1)} copy(bf16[16,44,8,128]{3,2,1,0:T(8,128)(2,1)} %get-tuple-element.34) | data formatting | bytes 2883584 | tf_op jit(solution)/shard_map/reshape | solution.py:308
  252.0 1.5 copy.156
  253.5 1.5 reshape_reshape.204
  (92 shorter events, 4.6 us)
Async XLA Ops:
  7.2 136.3 %reduce-scatter.4.cloned.1.call-start = ((), (), s32[]{:S(2)}) async-start(), calls=%async_computation.2 | async-start | bytes 10201088
  7.2 1.8 copy-start.3
  9.4 3.6 %copy-start.17 = (bf16[1,256]{1,0:T(2,128)(2,1)S(1)}, bf16[1,256]{1,0:T(2,128)(2,1)}, u32[]{:S(2)}) copy-start(bf16[1,256]{1,0:T(2,128)(2,1)} %param.21) | copy-start | bytes 1540
  9.4 3.7 %copy-start.18 = (bf16[1,256]{1,0:T(2,128)(2,1)S(1)}, bf16[1,256]{1,0:T(2,128)(2,1)}, u32[]{:S(2)}) copy-start(bf16[1,256]{1,0:T(2,128)(2,1)} %param.18) | copy-start | bytes 1540
  9.4 3.8 %copy-start.19 = (bf16[1,256]{1,0:T(2,128)(2,1)S(1)}, bf16[1,256]{1,0:T(2,128)(2,1)}, u32[]{:S(2)}) copy-start(bf16[1,256]{1,0:T(2,128)(2,1)} %param.14) | copy-start | bytes 1540
  24.7 1.3 copy-start.4
  24.7 213.0 %all-gather.3.cloned.1.call-start = ((), (), s32[]{:S(2)}) async-start(), calls=%async_computation.1 | async-start | bytes 10201088 | tf_op jit(solution)/shard_map/all_gather | solution.py:300
  30.8 3.1 %copy-start.5 = (f32[1,299056]{1,0:T(1,128)S(1)}, f32[1,299056]{1,0:T(1,128)}, u32[]{:S(2)}) copy-start(f32[1,299056]{1,0:T(1,128)} %param.27) | copy-start | bytes 3588676
  47.9 3.4 %copy-start.6 = (f32[1,128,352]{1,2,0:T(8,128)S(1)}, f32[1,128,352]{1,2,0:T(8,128)}, u32[]{:S(2)}) copy-start(f32[1,128,352]{1,2,0:T(8,128)} %copy.101) | copy-start | bytes 540676
  51.3 11.6 %copy-start.7 = (f32[1,128,352]{1,2,0:T(8,128)S(1)}, f32[1,128,352]{1,2,0:T(8,128)}, u32[]{:S(2)}) copy-start(f32[1,128,352]{1,2,0:T(8,128)} %copy.118) | copy-start | bytes 540676
  51.3 11.6 %copy-start.9 = (f32[1,45056]{1,0:T(1,128)S(1)}, f32[1,45056]{1,0:T(1,128)}, u32[]{:S(2)}) copy-start(f32[1,45056]{1,0:T(1,128)} %get-tuple-element.88) | copy-start | bytes 540676
  51.3 11.6 %copy-start.10 = (f32[1,16,8,2,128]{4,2,3,1,0:T(8,128)S(1)}, f32[1,16,8,2,128]{4,2,3,1,0:T(8,128)}, u32[]{:S(2)}) copy-start(f32[1,16,8,2,128]{4,2,3,1,0:T(8,128)} %copy.112) | copy-start | bytes 393220
  51.4 11.6 %copy-start.11 = (f32[1,16,8,2,128]{4,2,3,1,0:T(8,128)S(1)}, f32[1,16,8,2,128]{4,2,3,1,0:T(8,128)}, u32[]{:S(2)}) copy-start(f32[1,16,8,2,128]{4,2,3,1,0:T(8,128)} %copy.113) | copy-start | bytes 393220
  51.4 11.6 %copy-start.12 = (f32[1,16,8,2,128]{4,2,3,1,0:T(8,128)S(1)}, f32[1,16,8,2,128]{4,2,3,1,0:T(8,128)}, u32[]{:S(2)}) copy-start(f32[1,16,8,2,128]{4,2,3,1,0:T(8,128)} %copy.114) | copy-start | bytes 393220
  51.4 11.6 %copy-start.13 = (f32[1,16,8,2,128]{4,2,3,1,0:T(8,128)S(1)}, f32[1,16,8,2,128]{4,2,3,1,0:T(8,128)}, u32[]{:S(2)}) copy-start(f32[1,16,8,2,128]{4,2,3,1,0:T(8,128)} %copy.115) | copy-start | bytes 393220
  51.4 11.6 %copy-start.14 = (f32[1,2,8,16,128]{4,2,3,1,0:T(8,128)S(1)}, f32[1,2,8,16,128]{4,2,3,1,0:T(8,128)}, u32[]{:S(2)}) copy-start(f32[1,2,8,16,128]{4,2,3,1,0:T(8,128)} %copy.116) | copy-start | bytes 393220
  63.0 0.9 copy-start.8
  63.0 1.0 copy-start.15
  63.0 1.0 copy-start.16
  185.1 6.2 %copy-start.2 = (bf16[1,2344,128]{2,1,0:T(8,128)(2,1)S(1)}, bf16[1,2344,128]{2,1,0:T(8,128)(2,1)}, u32[]{:S(2)}) copy-start(bf16[1,2344,128]{2,1,0:T(8,128)(2,1)} %reduce-scatter.4.cloned.1.call-done) | copy-start | bytes 1800196
  192.8 1.0 copy-start.1
  202.4 6.3 %copy-start = (f32[2344,128]{1,0:T(8,128)S(1)}, f32[2344,128]{1,0:T(8,128)}, u32[]{:S(2)}) copy-start(f32[2344,128]{1,0:T(8,128)} %get-tuple-element.52) | copy-start | bytes 3600388
Sparse Core Ops, SparseCore 0:
  24.9 118.5 reduce-scatter.3
  163.5 74.2 all-gather.2

commit v2 on v1

--- a/solution.py
+++ b/solution.py
@@ -135,32 +135,32 @@
 
 def pack_kernel(plan, *refs):
     out_ref = refs[-1]
-    owners = out_ref.shape[0]
-
-    def body(j, carry):
-        for index, (r0, a, b, raw) in enumerate(plan):
-            src = refs[index]
-            if raw:
-                start = pl.multiple_of(j * a, a)
-                for rt in range(a // 8):
-                    for ct in range(b // 128):
-                        at = r0 + (rt * (b // 128) + ct) * 8
-                        out_ref[j, at : at + 8, :] = src[
-                            0, pl.ds(start + rt * 8, 8), ct * 128 : (ct + 1) * 128
-                        ]
-            else:
-                out_ref[j, r0 : r0 + a, :] = src[j]
-        return carry
-
-    lax.fori_loop(0, owners, body, 0)
+    for index, (r0, a, b, raw) in enumerate(plan):
+        src = refs[index]
+        if raw:
+            for rt in range(a // 8):
+                for ct in range(b // 128):
+                    at = r0 + (rt * (b // 128) + ct) * 8
+                    out_ref[0, at : at + 8, :] = src[
+                        0, rt * 8 : (rt + 1) * 8, ct * 128 : (ct + 1) * 128
+                    ]
+        else:
+            out_ref[0, r0 : r0 + a, :] = src[0]
 
 
 def pack_rows(inputs, plan, owners, rows):
+    specs = []
+    for x, (r0, a, b, raw) in zip(inputs, plan):
+        if raw:
+            specs.append(pl.BlockSpec((1, a, b), lambda j: (0, j, 0)))
+        else:
+            specs.append(pl.BlockSpec((1, a, 128), lambda j: (j, 0, 0)))
     return pl.pallas_call(
         functools.partial(pack_kernel, plan),
+        grid=(owners,),
         out_shape=jax.ShapeDtypeStruct((owners, rows, 128), jnp.bfloat16),
-        in_specs=[pl.BlockSpec(memory_space=pltpu.VMEM)] * len(inputs),
-        out_specs=pl.BlockSpec(memory_space=pltpu.VMEM),
+        in_specs=specs,
+        out_specs=pl.BlockSpec((1, rows, 128), lambda j: (j, 0, 0)),
     )(*inputs)
 
 

time: 263 us -> 268 us (1.019)
  Pallas kernels: 25 us -> 29.1 us
    pallas_call x1, Pallas kernels: 8.35 us -> 12.5 us  [pack_rows(): pl.pallas_call(functools.partial(pack_kernel, plan), grid=(owners,), out_...]
where the time goes in v2:
time: 268 us; the launch traced here: 266 us
  local copies, waits for them, and re-layouts  128 us (48%)
  waiting for transfers between devices  89.3 us (33%)
  Pallas kernels  29.1 us (11%)
  between operations  14.5 us (5%)
  other arithmetic  4.99 us (2%)
    unnamed x3, waiting for transfers between devices  76.6 us
    concatenate x3, local copies, waits for them, and re-layouts, to_flat(): return jnp.concatenate(out).reshape(1, -1)  31.6 us
    reshape x3, local copies, waits for them, and re-layouts, to_flat(): return jnp.concatenate(out).reshape(1, -1)  18.8 us
    pallas_call x1, Pallas kernels, apply_step(): pl.pallas_call(functools.partial(apply_kernel, nd, nt, segments), out_sha...  16.6 us
    concatenate x3, local copies, waits for them, and re-layouts, to_packed(): return jnp.concatenate(out, axis=0)  14.5 us
    all_gather x1, waiting for transfers between devices, on_device(): gathered = lax.all_gather(rounded, 'dp', axis=0, tiled=False)  12.7 us
    pallas_call x1, Pallas kernels, pack_rows(): pl.pallas_call(functools.partial(pack_kernel, plan), grid=(owners,), out_...  12.5 us
    slice x5, local copies, waits for them, and re-layouts, to_packed(): seg = row[starts[k]:starts[k] + piece_len[k]].reshape((1,) + blocks[k])  11.5 us
  transfers between devices with their start and end apart: 2, of which 2 were waited for; matrix products, arithmetic and copies ran while one was open for 38% of the time, Pallas kernels for 0%

profile of v2, /device:TPU:1, one launch (start us, length us, event | category | flops | bytes accessed | tf_op | source)
XLA Modules:
  0.0 266.0 jit_solution(4436104685132701770)
XLA Ops:
  7.2 1.8 copy.151
  9.1 0.3 copy.150
  9.5 3.5 %reshape_reshape_squeeze.3.refs_7_ = bf16[16,352,128]{2,1,0:T(8,128)(2,1)} reshape(bf16[1,352,2048]{2,1,0:T(8,128)(2,1)} %param.24) | data formatting | bytes 2883584 | tf_op jit(solution)/shard_map/reshape;reshape;squeeze | solution.py:214
  13.4 2.3 copy_bitcast_fusion.2
  15.7 0.6 pad.9.refs_8_
  16.4 12.5 %shard_map.245 = bf16[16,2344,128]{2,1,0:T(8,128)(2,1)} custom-call(bf16[1,2048,256]{2,1,0:T(8,128)(2,1)} %refs_0_.1, bf16[1,2048,256]{2,1,0:T(8,128)(2,1)} %refs_1_.1, bf16[1,2048,256]{2,1,0:T(8,128)(2,1)} %refs_2_.1, bf16[1,2048,256]{2,1,0:T(8,128)(2,1)} %refs_3_.1, bf16[1,256,2048]{2,1,0:T(8,128)(2,1)} %refs_4_.1, ...), custom_call_target="tpu_custom_call" | custom-call | tf_op jit(solution)/shard_map/pallas_call | solution.py:158
  28.9 1.2 copy-done.4
  30.1 1.4 fusion.21
  31.5 0.7 copy.95
  32.2 0.7 copy.96
  32.9 0.7 copy.97
  33.5 0.7 copy.98
  34.2 0.7 copy.99
  34.9 1.9 slice_reduce_fusion.4
  37.2 0.8 copy.101
  38.0 1.4 fusion.20
  39.4 0.7 copy.112
  40.0 0.7 copy.113
  40.7 0.7 copy.114
  41.3 0.7 copy.115
  42.0 0.7 copy.116
  42.7 4.2 %slice_reduce_fusion = (f32[45056]{0:T(1024)S(1)}, f32[45056]{0:T(1024)S(1)}, f32[1,45056]{1,0:T(1,128)}, f32[1,45056]{1,0:T(1,128)}, f32[45056]{0:T(1024)S(1)}, /*index=5*/f32[45056]{0:T(1024)S(1)}) fusion(f32[1,299056]{1,0:T(1,128)S(1)} %copy-done.5, f32[1,299056]{1,0:T(1,128)} %param.26), kind=kLoop, calls=%fused_computation.26 | loop fusion | bytes 2162688 | tf_op jit(solution)/shard_map/slice | solution.py:264
  47.3 0.8 copy.118
  48.1 2.6 fusion.19
  50.7 0.7 copy.102
  51.4 0.7 copy.103
  52.0 0.7 copy.104
  52.7 0.6 copy.105
  53.3 0.7 copy.106
  54.6 0.8 slice_bitcast_fusion.22
  55.5 11.5 %concatenate.31.weight_ref = f32[2344,128]{1,0:T(8,128)} concatenate(f32[256,128]{1,0:T(8,128)} %bitcast.341, f32[256,128]{1,0:T(8,128)} %bitcast.342, f32[256,128]{1,0:T(8,128)} %bitcast.343, f32[256,128]{1,0:T(8,128)} %bitcast.344, f32[256,128]{1,0:T(8,128)} %bitcast.345, f32[352,128]{1,0:T(8,128)S(1)} %bitcast.287, f32[352,128]{1,0:T(8,128)S(1)} %bitcast.288, ...), dimensions={0} | concatenate | bytes 2400256 | tf_op jit(solution)/shard_map/concatenate | solution.py:270
  67.2 0.8 copy-done.8
  68.2 2.8 %concatenate.33 = f32[2344,128]{1,0:T(8,128)S(1)} concatenate(f32[256,128]{1,0:T(8,128)S(1)} %bitcast.351, f32[256,128]{1,0:T(8,128)S(1)} %bitcast.352, f32[256,128]{1,0:T(8,128)} %bitcast.353, f32[256,128]{1,0:T(8,128)} %bitcast.354, f32[256,128]{1,0:T(8,128)} %bitcast.355, f32[352,128]{1,0:T(8,128)S(1)} %bitcast.291, f32[352,128]{1,0:T(8,128)S(1)} %bitcast.292, ...), dimensions={0} | concatenate | bytes 2400256 | tf_op jit(solution)/shard_map/concatenate | solution.py:270
  71.0 76.6 %reduce-scatter.4.cloned.1.call-done = bf16[1,2344,128]{2,1,0:T(8,128)(2,1)} async-done(((bf16[16,2344,128]{2,1,0:T(8,128)(2,1)}), bf16[1,2344,128]{2,1,0:T(8,128)(2,1)}) %reduce-scatter.4.cloned.1.call-update) | async-done | bytes 600080
  147.6 3.3 %add_select_fusion.update_ref = f32[2344,128]{1,0:T(8,128)} fusion(f32[2344,128]{1,0:T(8,128)} %concatenate.31.weight_ref, f32[2344,128]{1,0:T(8,128)S(1)} %concatenate.36, f32[2344,128]{1,0:T(8,128)S(1)} %concatenate.33, s32[2344]{0:T(1024)S(1)} %iota_multiply_fusion, bf16[1,2344,128]{2,1,0:T(8,128)(2,1)} %reduce-scatter.4.cloned.1.call-done), kind=kLoop, calls=%fused_computation.1 | loop fusion | flops 4500480 | bytes 5409952 | tf_op jit(solution)/shard_map/jit(_where)/select_n | solution.py:295
  150.9 16.6 %shard_map.246 = (f32[2344,128]{1,0:T(8,128)}, bf16[2344,128]{1,0:T(8,128)(2,1)}) custom-call(f32[2344,128]{1,0:T(8,128)} %concatenate.31.weight_ref, f32[2344,128]{1,0:T(8,128)} %add_select_fusion.update_ref), custom_call_target="tpu_custom_call" | custom-call | tf_op jit(solution)/shard_map/pallas_call | solution.py:170
  167.5 1.2 fusion.18
  169.0 0.7 copy.122
  169.7 0.7 copy.123
  170.4 1.1 slice_bitcast_fusion.8
  171.9 0.2 reshape.211
  172.1 0.9 slice_bitcast_fusion.17
  173.0 16.3 %concatenate.37 = f32[299056]{0:T(1024)} concatenate(f32[16]{0:T(128)S(1)} %get-tuple-element.70, f32[32768]{0:T(1024)S(1)} %bitcast.296, f32[32768]{0:T(1024)S(1)} %bitcast.299, f32[32768]{0:T(1024)S(1)} %bitcast.302, f32[16]{0:T(128)S(1)} %get-tuple-element.69, f32[32768]{0:T(1024)} %bitcast.305, f32[32768]{0:T(1024)} %bitcast.308, f32[16]{0:T(128)S(1)} %get-tuple-element.68, ...), dimensions={0} | concatenate | bytes 2392448 | tf_op jit(solution)/shard_map/concatenate | solution.py:281
  189.3 6.2 %reshape.212 = f32[1,299056]{1,0:T(1,128)} reshape(f32[299056]{0:T(1024)} %concatenate.37) | data formatting | bytes 2392448 | tf_op jit(solution)/shard_map/reshape | solution.py:281
  195.5 1.4 fusion.4
  197.3 0.6 copy-done.1
  198.1 0.2 reshape.214
  198.4 0.2 reshape.216
  198.6 0.9 slice_bitcast_fusion.14
  199.5 7.0 %concatenate.38 = f32[299056]{0:T(1024)S(1)} concatenate(f32[16]{0:T(128)S(1)} %get-tuple-element.59, f32[32768]{0:T(1024)S(1)} %bitcast.297, f32[32768]{0:T(1024)S(1)} %bitcast.300, f32[32768]{0:T(1024)S(1)} %bitcast.303, f32[16]{0:T(128)S(1)} %get-tuple-element.58, f32[32768]{0:T(1024)S(1)} %bitcast.306, f32[32768]{0:T(1024)S(1)} %bitcast.309, f32[16]{0:T(128)S(1)} %get-tuple-element.57, ...), dimensions={0} | concatenate | bytes 2392448 | tf_op jit(solution)/shard_map/concatenate | solution.py:281
  206.5 6.3 %reshape.217 = f32[1,299056]{1,0:T(1,128)} reshape(f32[299056]{0:T(1024)S(1)} %concatenate.38) | data formatting | bytes 2392448 | tf_op jit(solution)/shard_map/reshape | solution.py:281
  213.2 0.7 copy.137
  214.6 8.3 %concatenate.39 = f32[299056]{0:T(1024)S(1)} concatenate(f32[16]{0:T(128)S(1)} %get-tuple-element.46, f32[32768]{0:T(1024)S(1)} %bitcast.298, f32[32768]{0:T(1024)S(1)} %bitcast.301, f32[32768]{0:T(1024)S(1)} %bitcast.304, f32[16]{0:T(128)S(1)} %get-tuple-element.45, f32[32768]{0:T(1024)S(1)} %bitcast.307, f32[32768]{0:T(1024)} %bitcast.310, f32[16]{0:T(128)S(1)} %get-tuple-element.44, ...), dimensions={0} | concatenate | bytes 2392448 | tf_op jit(solution)/shard_map/concatenate | solution.py:281
  222.9 6.3 %reshape.222 = f32[1,299056]{1,0:T(1,128)} reshape(f32[299056]{0:T(1024)S(1)} %concatenate.39) | data formatting | bytes 2392448 | tf_op jit(solution)/shard_map/reshape | solution.py:281
  229.2 12.7 %all-gather.3.cloned.1.call-done = bf16[37504,128]{1,0:T(8,128)(2,1)} async-done(((bf16[2344,128]{1,0:T(8,128)(2,1)}), bf16[37504,128]{1,0:T(8,128)(2,1)}) %all-gather.3.cloned.1.call-update) | async-done | bytes 9601040 | tf_op jit(solution)/shard_map/all_gather | solution.py:300
  241.9 1.0 slice_reduce_fusion.6
  242.9 5.0 %fusion.15 = (bf16[16,256,128]{2,1,0:T(8,128)(2,1)}, bf16[16,256,128]{2,1,0:T(8,128)(2,1)}, bf16[16,256,128]{2,1,0:T(8,128)(2,1)}, bf16[16,256,128]{2,1,0:T(8,128)(2,1)}, bf16[16,256,128]{2,1,0:T(8,128)(2,1)}) fusion(bf16[16,2344,128]{2,1,0:T(8,128)(2,1)} %bitcast.274), kind=kLoop, calls=%fused_computation.68 | loop fusion | bytes 10485760 | tf_op jit(solution)/shard_map/slice | solution.py:305
  247.9 3.7 %fusion.14 = (bf16[16,352,128]{2,1,0:T(8,128)(2,1)S(1)}, bf16[16,44,8,128]{3,2,1,0:T(8,128)(2,1)}, bf16[16,44,8,128]{3,2,1,0:T(8,128)(2,1)S(1)}) fusion(bf16[16,2344,128]{2,1,0:T(8,128)(2,1)} %bitcast.275), kind=kLoop, calls=%fused_computation.67 | loop fusion | bytes 8650752 | tf_op jit(solution)/shard_map/slice | solution.py:305
  251.5 0.6 reshape_squeeze.17
  252.1 0.6 reshape_squeeze.18
  252.7 0.6 reshape_squeeze.19
  253.3 2.9 %copy.157 = bf16[16,44,8,128]{3,2,0,1:T(8,128)(2,1)} copy(bf16[16,44,8,128]{3,2,1,0:T(8,128)(2,1)} %get-tuple-element.34) | data formatting | bytes 2883584 | tf_op jit(solution)/shard_map/reshape | solution.py:308
  256.2 1.5 copy.156
  257.7 1.5 reshape_reshape.204
  (92 shorter events, 4.6 us)
Async XLA Ops:
  7.2 140.4 %reduce-scatter.4.cloned.1.call-start = ((), (), s32[]{:S(2)}) async-start(), calls=%async_computation.2 | async-start | bytes 10201088
  7.2 1.8 copy-start.3
  9.4 3.6 %copy-start.17 = (bf16[1,256]{1,0:T(2,128)(2,1)S(1)}, bf16[1,256]{1,0:T(2,128)(2,1)}, u32[]{:S(2)}) copy-start(bf16[1,256]{1,0:T(2,128)(2,1)} %param.21) | copy-start | bytes 1540
  9.4 3.7 %copy-start.18 = (bf16[1,256]{1,0:T(2,128)(2,1)S(1)}, bf16[1,256]{1,0:T(2,128)(2,1)}, u32[]{:S(2)}) copy-start(bf16[1,256]{1,0:T(2,128)(2,1)} %param.18) | copy-start | bytes 1540
  9.4 3.8 %copy-start.19 = (bf16[1,256]{1,0:T(2,128)(2,1)S(1)}, bf16[1,256]{1,0:T(2,128)(2,1)}, u32[]{:S(2)}) copy-start(bf16[1,256]{1,0:T(2,128)(2,1)} %param.14) | copy-start | bytes 1540
  28.8 1.3 copy-start.4
  28.9 213.0 %all-gather.3.cloned.1.call-start = ((), (), s32[]{:S(2)}) async-start(), calls=%async_computation.1 | async-start | bytes 10201088 | tf_op jit(solution)/shard_map/all_gather | solution.py:300
  34.9 3.1 %copy-start.5 = (f32[1,299056]{1,0:T(1,128)S(1)}, f32[1,299056]{1,0:T(1,128)}, u32[]{:S(2)}) copy-start(f32[1,299056]{1,0:T(1,128)} %param.27) | copy-start | bytes 3588676
  52.0 3.4 %copy-start.6 = (f32[1,128,352]{1,2,0:T(8,128)S(1)}, f32[1,128,352]{1,2,0:T(8,128)}, u32[]{:S(2)}) copy-start(f32[1,128,352]{1,2,0:T(8,128)} %copy.101) | copy-start | bytes 540676
  55.4 11.6 %copy-start.7 = (f32[1,128,352]{1,2,0:T(8,128)S(1)}, f32[1,128,352]{1,2,0:T(8,128)}, u32[]{:S(2)}) copy-start(f32[1,128,352]{1,2,0:T(8,128)} %copy.118) | copy-start | bytes 540676
  55.5 11.6 %copy-start.9 = (f32[1,45056]{1,0:T(1,128)S(1)}, f32[1,45056]{1,0:T(1,128)}, u32[]{:S(2)}) copy-start(f32[1,45056]{1,0:T(1,128)} %get-tuple-element.88) | copy-start | bytes 540676
  55.5 11.6 %copy-start.10 = (f32[1,16,8,2,128]{4,2,3,1,0:T(8,128)S(1)}, f32[1,16,8,2,128]{4,2,3,1,0:T(8,128)}, u32[]{:S(2)}) copy-start(f32[1,16,8,2,128]{4,2,3,1,0:T(8,128)} %copy.112) | copy-start | bytes 393220
  55.5 11.6 %copy-start.11 = (f32[1,16,8,2,128]{4,2,3,1,0:T(8,128)S(1)}, f32[1,16,8,2,128]{4,2,3,1,0:T(8,128)}, u32[]{:S(2)}) copy-start(f32[1,16,8,2,128]{4,2,3,1,0:T(8,128)} %copy.113) | copy-start | bytes 393220
  55.5 11.6 %copy-start.12 = (f32[1,16,8,2,128]{4,2,3,1,0:T(8,128)S(1)}, f32[1,16,8,2,128]{4,2,3,1,0:T(8,128)}, u32[]{:S(2)}) copy-start(f32[1,16,8,2,128]{4,2,3,1,0:T(8,128)} %copy.114) | copy-start | bytes 393220
  55.5 11.6 %copy-start.13 = (f32[1,16,8,2,128]{4,2,3,1,0:T(8,128)S(1)}, f32[1,16,8,2,128]{4,2,3,1,0:T(8,128)}, u32[]{:S(2)}) copy-start(f32[1,16,8,2,128]{4,2,3,1,0:T(8,128)} %copy.115) | copy-start | bytes 393220
  55.5 11.6 %copy-start.14 = (f32[1,2,8,16,128]{4,2,3,1,0:T(8,128)S(1)}, f32[1,2,8,16,128]{4,2,3,1,0:T(8,128)}, u32[]{:S(2)}) copy-start(f32[1,2,8,16,128]{4,2,3,1,0:T(8,128)} %copy.116) | copy-start | bytes 393220
  67.1 0.9 copy-start.8
  67.1 1.0 copy-start.15
  67.1 1.0 copy-start.16
  189.3 6.2 %copy-start.2 = (bf16[1,2344,128]{2,1,0:T(8,128)(2,1)S(1)}, bf16[1,2344,128]{2,1,0:T(8,128)(2,1)}, u32[]{:S(2)}) copy-start(bf16[1,2344,128]{2,1,0:T(8,128)(2,1)} %reduce-scatter.4.cloned.1.call-done) | copy-start | bytes 1800196
  196.9 1.0 copy-start.1
  206.5 6.3 %copy-start = (f32[2344,128]{1,0:T(8,128)S(1)}, f32[2344,128]{1,0:T(8,128)}, u32[]{:S(2)}) copy-start(f32[2344,128]{1,0:T(8,128)} %get-tuple-element.52) | copy-start | bytes 3600388
Sparse Core Ops, SparseCore 0:
  29.0 118.5 reduce-scatter.3
  167.6 74.2 all-gather.2
